TPU v7x, 512 devices: a whole 4x8x8 slice. The times are simulated.
512 devices in a mesh: blade: 256 (over z, y, x), inst: 2 (over core).
Axes of the slice: x: 4, y: 8, z: 8, core: 2. Of those that a mesh axis runs over, the one named last changes fastest.
Arguments:
- tangent_seed: float32 [256, 5, 24, 1024], P('blade', None, 'inst'), may hold values from -6 to 6
- adjoint_seed: float32 [256, 5, 24, 1024], P('blade', None, 'inst'), may hold values from -6 to 6
- jacobian: bfloat16 [256, 24, 25, 1024], P('blade', 'inst'), may hold values from -1 to 4
- precond: bfloat16 [256, 24, 25, 1024], P('blade', 'inst'), may hold values from -1 to 4
- upwind: float32 [256, 1024], P('blade'), may hold values from 0.2 to 1
- up_weight: float32 [256, 256], P('blade'), may hold values from 0.3 to 1.2
- bottom_face_strength: float32 [256, 256], P('blade'), may hold values from 0.3 to 1.2
- up_cells: int32 [256], replicated, may hold values from 0 to 1023, as said below
- lo_cells: int32 [256], replicated, may hold values from 0 to 1023, as said below
- phase_index: int32 [11], replicated, may hold values from 0 to 255
Outputs:
- tangent_out: float32 [256, 5, 24, 1024], P('blade', None, 'inst')
- adjoint_out: float32 [256, 5, 24, 1024], P('blade', None, 'inst')
Inputs may be any that keep to these rules, and one draw needn't show every extreme that they name: `up_cells`: entry f of the table is one of the cells 4 f to 4 f + 3. `lo_cells`: entry f of the table is one of the cells 4 f to 4 f + 3.
All inputs are finite; a program needn't handle non-finite values.
Results may differ from a plain program's by a relative error of at most 0.0003.
Values sent between devices are 32-bit elements; how exact they have to be, the bound alone decides.
No kernel may reach another device: no remote copies, remote signals or barrier semaphores. Data moves between devices by JAX's collectives and lax.ppermute only.
A program may use at most 64 MiB of HBM per device.

v0:
```python
import jax
import jax.numpy as jnp
from jax import lax
from jax.sharding import PartitionSpec as P

SNAPSHOT_COUNT = 24
NH = 11
OMEGA = 0.15


def passed_along(block, axis, distance):
    devices = range(lax.axis_size(axis))
    route = [((i - distance) % len(devices), i) for i in devices]
    return lax.ppermute(block, axis, route)


def spectral(phase_index, passages):
    sampled_moments = jnp.arange(SNAPSHOT_COUNT, dtype=jnp.int32)
    snapshot_displacement = sampled_moments[:, None] - sampled_moments[None, :]
    orders = jnp.arange(1, NH + 1, dtype=jnp.int32)
    wrapped = (
        jnp.mod(orders[:, None, None] * snapshot_displacement[None, :, :], SNAPSHOT_COUNT).astype(
            jnp.float32
        )
        / SNAPSHOT_COUNT
    )
    weights = orders.astype(jnp.float32)[:, None, None]
    skewed = -(2.0 / SNAPSHOT_COUNT) * jnp.sum(weights * jnp.sin(2.0 * jnp.pi * wrapped), axis=0)
    derivative = 0.5 * skewed - 0.5 * skewed.T
    phase_angle = phase_index.astype(jnp.float32)[:, None, None] / passages
    parity = 1.0 - 2.0 * jnp.mod(snapshot_displacement, 2).astype(jnp.float32)
    rotation = (1.0 + parity) / SNAPSHOT_COUNT + 2.0 / SNAPSHOT_COUNT * jnp.sum(
        jnp.cos(2.0 * jnp.pi * (wrapped - phase_angle)), axis=0
    )
    return (derivative, rotation)


def block_apply(blocks, vector):
    variables = vector.shape[1]
    result_rows = []
    for row_index in range(variables):
        summed = blocks[:, :, row_index * variables, :] * vector[:, 0]
        for column_index in range(1, variables):
            summed = (
                summed
                + blocks[:, :, row_index * variables + column_index, :] * vector[:, column_index]
            )
        result_rows.append(summed)
    return jnp.stack(result_rows, axis=1)


def block_apply_t(blocks, vector):
    variables = vector.shape[1]
    result_rows = []
    for column_index in range(variables):
        summed = blocks[:, :, column_index, :] * vector[:, 0]
        for row_index in range(1, variables):
            summed = (
                summed
                + blocks[:, :, row_index * variables + column_index, :] * vector[:, row_index]
            )
        result_rows.append(summed)
    return jnp.stack(result_rows, axis=1)


def instance_mix(matrix, vector):
    return jnp.einsum("ts,pvsc->pvtc", matrix, vector, precision=lax.Precision.HIGHEST)


def cell_mask(cells_table):
    face_count = cells_table.shape[0]
    within = cells_table - 4 * jnp.arange(face_count, dtype=jnp.int32)
    spread = jnp.repeat(within, 4)
    slot_in_group = jnp.mod(jnp.arange(4 * face_count, dtype=jnp.int32), 4)
    return (spread == slot_in_group).astype(jnp.float32)


def face_pick(vector, mask):
    lead = vector.shape[:-1]
    picked = (vector * mask).reshape(lead + (vector.shape[-1] // 4, 4))
    return jnp.sum(picked, axis=-1)


def face_spread(values, mask):
    return jnp.repeat(values, 4, axis=-1) * mask


def regroup(vector, lo_mask, up_mask, derivative, rotation):
    lo_face = face_pick(vector, lo_mask)
    up_face = face_pick(vector, up_mask)
    own_count = vector.shape[2]
    first_row = lax.axis_index("inst") * own_count
    own_deriv = lax.dynamic_slice_in_dim(derivative, first_row, own_count, 0)
    own_rot = lax.dynamic_slice_in_dim(rotation, first_row, own_count, 0)
    own_rot_t = lax.dynamic_slice_in_dim(rotation.T, first_row, own_count, 0)
    return (
        instance_mix(own_deriv, lax.all_gather(vector, "inst", axis=2, tiled=True)),
        instance_mix(own_rot, lax.all_gather(lo_face, "inst", axis=2, tiled=True)),
        instance_mix(own_rot_t, lax.all_gather(up_face, "inst", axis=2, tiled=True)),
    )


def cycle_faces(next_source, previous_source_term):
    from_next = jnp.concatenate([next_source[1:], passed_along(next_source, "blade", -1)], axis=0)
    from_prev = jnp.concatenate(
        [passed_along(previous_source_term, "blade", 1), previous_source_term[:-1]], axis=0
    )
    return (from_next, from_prev)


def on_device(
    tangent_seed,
    adjoint_seed,
    jacobian,
    precond,
    upwind,
    up_weight,
    bottom_face_strength,
    up_cells,
    lo_cells,
    phase_index,
):
    passages = tangent_seed.shape[0] * lax.axis_size("blade")
    derivative, rotation = spectral(phase_index, passages)
    up_mask = cell_mask(up_cells)
    lo_mask = cell_mask(lo_cells)
    dual_field = block_apply_t(precond, adjoint_seed)
    negated = -dual_field
    up_scale = up_weight[:, None, None, :]
    lo_scale = bottom_face_strength[:, None, None, :]
    timed_tan, lo_tan, up_tan = regroup(tangent_seed, lo_mask, up_mask, derivative, rotation)
    next_tan, previous_tangent = cycle_faces(lo_tan, up_tan)
    timed_adj, lo_adj, up_adj = regroup(negated, lo_mask, up_mask, derivative, rotation)
    next_adj, prev_adj = cycle_faces(-lo_scale * lo_adj, -up_scale * up_adj)
    shifted = jnp.pad(tangent_seed[..., :-1], ((0, 0), (0, 0), (0, 0), (1, 0)))
    applied = (
        block_apply(jacobian, tangent_seed) - upwind[:, None, None, :] * shifted + OMEGA * timed_tan
    )
    applied = (
        applied
        - face_spread(up_scale * next_tan, up_mask)
        - face_spread(lo_scale * previous_tangent, lo_mask)
    )
    tangent_out = block_apply(precond, applied)
    shifted = jnp.pad(
        (upwind[:, None, None, :] * dual_field)[..., 1:], ((0, 0), (0, 0), (0, 0), (0, 1))
    )
    adjoint_out = block_apply_t(jacobian, dual_field) - shifted + OMEGA * timed_adj
    adjoint_out = adjoint_out - face_spread(prev_adj, lo_mask) - face_spread(next_adj, up_mask)
    return (tangent_out, adjoint_out)


def solution(mesh):
    in_specs = (
        P("blade", None, "inst", None),
        P("blade", None, "inst", None),
        P("blade", "inst", None, None),
        P("blade", "inst", None, None),
        P("blade", None),
        P("blade", None),
        P("blade", None),
        P(),
        P(),
        P(),
    )
    out_specs = (P("blade", None, "inst", None), P("blade", None, "inst", None))
    return jax.shard_map(
        on_device, mesh=mesh, in_specs=in_specs, out_specs=out_specs, check_vma=False
    )
```

profile of v0, /device:TPU:1, one launch (start us, length us, event | category | flops | bytes accessed | tf_op | source)
XLA Modules:
  0.0 108.2 jit_solution(11999192427864549714)
XLA Ops:
  2.5 1.8 %fusion.170 = (f32[1,5,12,1024]{3,2,1,0:T(8,128)S(1)}, f32[1,5,12,1024]{3,2,1,0:T(8,128)S(1)}, f32[1,5,12,1024]{3,2,1,0:T(8,128)}) fusion(f32[1,5,12,1024]{3,0,2,1:T(1,128)} %param.10, f32[1024]{0:T(1024)S(1)} %get-tuple-element.88, f32[1024]{0:T(1024)S(1)} %get-tuple-element.89), kind=kLoop, calls=%fused_computation.354 | loop fusion | flops 122880 | bytes 991232 | tf_op args[0]
  4.3 1.7 %copy.312 = f32[1,5,12,1024]{2,3,1,0:T(8,128)S(1)} copy(f32[1,5,12,1024]{3,2,1,0:T(8,128)} %get-tuple-element.77) | data formatting | bytes 491520 | tf_op jit(solution)/shard_map/mul | solution.py:80
  6.0 2.9 %reduce_sum.66 = f32[5,12,256]{1,2,0:T(8,128)} reduce(f32[5,12,256,4]{1,3,2,0:T(4,128)S(1)} %bitcast.467, f32[]{:T(128)} %constant.66.clone.1), dimensions={3}, to_apply=%region_3.4 | reduce | flops 46080 | bytes 307204 | tf_op jit(solution)/shard_map/reduce_sum | solution.py:81
  8.9 1.4 %copy.313 = f32[5,12,256]{2,0,1:T(8,128)S(1)} copy(f32[5,12,256]{1,2,0:T(8,128)} %reduce_sum.66) | data formatting | bytes 122880 | tf_op jit(solution)/shard_map/reduce_sum | solution.py:81
  10.3 8.5 %all-gather.1 = f32[5,24,256]{2,0,1:T(8,128)S(1)} all-gather(f32[5,12,256]{2,0,1:T(8,128)S(1)} %copy.313), channel_id=3, replica_groups=mesh['blade'=256,'inst'=2] {'inst'}, dimensions={1}, use_global_device_ids=true | all-gather | bytes 184320 | tf_op jit(solution)/shard_map/all_gather | solution.py:99
  18.8 1.7 %multiply_reduce_fusion.2 = (f32[24,24]{1,0:T(8,128)}, f32[24,24]{1,0:T(8,128)S(1)}) fusion(s32[24,24]{1,0:T(8,128)S(1)} %iota_subtract_fusion, s32[11]{0:T(128)S(1)} %get-tuple-element.90, f32[11]{0:T(128)S(1)} %get-tuple-element.91, f32[11]{0:T(128)S(1)} %convert_multiply_fusion.75), kind=kLoop, calls=%fused_computation.31 | loop fusion | flops 93888 | bytes 7044 | tf_op jit(solution)/shard_map/reduce_sum | solution.py:28
  20.5 1.0 convolution_bitcast_fusion.2
  21.5 1.9 %collective-permute-start.1 = (f32[1,5,12,256]{3,2,1,0:T(8,128)}, f32[1,5,12,256]{3,2,1,0:T(8,128)}, u32[]{:S(2)}, u32[]{:S(2)}) collective-permute-start(f32[1,5,12,256]{3,2,1,0:T(8,128)} %convolution_bitcast_fusion.2), channel_id=1, source_target_pairs={{510,0},{0,2},{2,4},{4,6},{6,8},{8,10},{10,12},{12,14},{14,16},{16... | collective-permute-start | bytes 184328 | tf_op jit(solution)/shard_map/ppermute | solution.py:14
  24.2 2.9 %reduce_sum.63 = f32[5,12,256]{1,2,0:T(8,128)} reduce(f32[5,12,256,4]{1,3,2,0:T(4,128)S(1)} %bitcast.466, f32[]{:T(128)} %constant.66.clone.1), dimensions={3}, to_apply=%region_1.2 | reduce | flops 46080 | bytes 307204 | tf_op jit(solution)/shard_map/reduce_sum | solution.py:81
  27.0 1.5 %copy.307 = f32[5,12,256]{2,0,1:T(8,128)S(1)} copy(f32[5,12,256]{1,2,0:T(8,128)} %reduce_sum.63) | data formatting | bytes 122880 | tf_op jit(solution)/shard_map/reduce_sum | solution.py:81
  28.5 1.9 %all-gather = f32[5,24,256]{2,0,1:T(8,128)S(1)} all-gather(f32[5,12,256]{2,0,1:T(8,128)S(1)} %copy.307), channel_id=2, replica_groups=mesh['blade'=256,'inst'=2] {'inst'}, dimensions={1}, use_global_device_ids=true | all-gather | bytes 184320 | tf_op jit(solution)/shard_map/all_gather | solution.py:98
  30.5 0.9 convolution_bitcast_fusion.3
  31.4 10.7 %collective-permute-start = (f32[1,5,12,256]{3,2,1,0:T(8,128)}, f32[1,5,12,256]{3,2,1,0:T(8,128)}, u32[]{:S(2)}, u32[]{:S(2)}) collective-permute-start(f32[1,5,12,256]{3,2,1,0:T(8,128)} %convolution_bitcast_fusion.3), channel_id=1, source_target_pairs={{2,0},{4,2},{6,4},{8,6},{10,8},{12,10},{14,12},{16,14},{18,16},{20... | collective-permute-start | bytes 184328 | tf_op jit(solution)/shard_map/ppermute | solution.py:14
  42.1 2.1 %fusion.168 = (bf16[1,12,1,1024]{3,2,1,0:T(2,128)(2,1)S(1)}, bf16[1,12,1,1024]{3,2,1,0:T(2,128)(2,1)S(1)}, bf16[1,12,1,1024]{3,2,1,0:T(2,128)(2,1)S(1)}, bf16[1,...) fusion(bf16[1,12,25,1024]{3,2,1,0:T(8,128)(2,1)} %param.12), kind=kLoop, calls=%fused_computation.352 | loop fusion | bytes 294912 | tf_op jit(solution)/shard_map/slice | solution.py:42
  44.1 4.7 %fusion.167 = (bf16[1,12,1,1024]{3,2,1,0:T(2,128)(2,1)}, bf16[1,12,1,1024]{3,2,1,0:T(2,128)(2,1)}, bf16[1,12,1,1024]{3,2,1,0:T(2,128)(2,1)}, bf16[1,12,1,1024]{3...) fusion(bf16[1,12,25,1024]{3,2,1,0:T(8,128)(2,1)} %param.12), kind=kLoop, calls=%fused_computation.351 | loop fusion | bytes 933888 | tf_op jit(solution)/shard_map/slice | solution.py:46
  49.2 1.0 fusion.165
  50.6 0.9 fusion.40
  55.3 2.4 %all-gather.3 = f32[5,24,256]{2,0,1:T(8,128)S(1)} all-gather(f32[5,12,256]{2,0,1:T(8,128)S(1)} %copy.368), channel_id=5, replica_groups=mesh['blade'=256,'inst'=2] {'inst'}, dimensions={1}, use_global_device_ids=true | all-gather | bytes 184320 | tf_op jit(solution)/shard_map/all_gather | solution.py:98
  58.6 3.6 %collective-permute-start.3 = (f32[1,5,12,256]{3,2,1,0:T(8,128)}, f32[1,5,12,256]{3,2,1,0:T(8,128)}, u32[]{:S(2)}, u32[]{:S(2)}) collective-permute-start(f32[1,5,12,256]{3,2,1,0:T(8,128)} %fusion.11), channel_id=1, source_target_pairs={{2,0},{4,2},{6,4},{8,6},{10,8},{12,10},{14,12},{16,14},{18,16},{20... | collective-permute-start | bytes 184328 | tf_op jit(solution)/shard_map/ppermute | solution.py:14
  62.3 2.4 %all-gather.2 = f32[5,24,256]{2,0,1:T(8,128)S(1)} all-gather(f32[5,12,256]{2,0,1:T(8,128)S(1)} %copy.361), channel_id=4, replica_groups=mesh['blade'=256,'inst'=2] {'inst'}, dimensions={1}, use_global_device_ids=true | all-gather | bytes 184320 | tf_op jit(solution)/shard_map/all_gather | solution.py:99
  64.6 1.0 fusion.9
  65.6 2.0 %collective-permute-start.2 = (f32[1,5,12,256]{3,2,1,0:T(8,128)}, f32[1,5,12,256]{3,2,1,0:T(8,128)}, u32[]{:S(2)}, u32[]{:S(2)}) collective-permute-start(f32[1,5,12,256]{3,2,1,0:T(8,128)} %fusion.9), channel_id=1, source_target_pairs={{510,0},{0,2},{2,4},{4,6},{6,8},{8,10},{10,12},{12,14},{14,16},{16... | collective-permute-start | bytes 184328 | tf_op jit(solution)/shard_map/ppermute | solution.py:14
  67.7 2.2 %all_gather.18 = f32[1,5,24,1024]{3,0,1,2:T(1,128)S(1)} all-gather(f32[1,5,12,1024]{3,0,1,2:T(1,128)S(1)} %copy.303), channel_id=1, replica_groups=mesh['blade'=256,'inst'=2] {'inst'}, dimensions={2}, use_global_device_ids=true | all-gather | bytes 737280 | tf_op jit(solution)/shard_map/all_gather | solution.py:97
  71.3 0.9 fusion.70
  72.2 0.9 fusion.75
  73.1 0.9 fusion.90
  74.1 0.9 fusion.80
  77.0 2.5 %all_gather.21 = f32[1,5,24,1024]{3,0,1,2:T(1,128)} all-gather(f32[1,5,12,1024]{3,0,1,2:T(1,128)S(1)} %copy.347), channel_id=1, replica_groups=mesh['blade'=256,'inst'=2] {'inst'}, dimensions={2}, use_global_device_ids=true | all-gather | bytes 737280 | tf_op jit(solution)/shard_map/all_gather | solution.py:97
  79.6 0.9 slice_multiply_fusion
  80.6 0.9 multiply_bitcast_fusion
  81.5 1.1 %copy.316 = f32[5,12,256]{1,2,0:T(8,128)} copy(f32[5,12,256]{2,1,0:T(8,128)S(1)} %multiply_bitcast_fusion) | data formatting | bytes 122880 | tf_op jit(solution)/shard_map/mul | solution.py:142
  82.7 1.5 %broadcast_in_dim.48 = f32[5,12,256,4]{1,3,2,0:T(4,128)S(1)} broadcast(f32[5,12,256]{1,2,0:T(8,128)} %copy.316), dimensions={0,1,2} | broadcast | bytes 307200 | tf_op jit(solution)/shard_map/broadcast_in_dim | solution.py:85
  84.2 1.5 %copy.317 = f32[1,5,12,1024]{3,2,1,0:T(8,128)} copy(f32[1,5,12,1024]{2,3,1,0:T(8,128)S(1)} %bitcast.468) | data formatting | bytes 491520 | tf_op jit(solution)/shard_map/broadcast_in_dim | solution.py:85
  85.7 0.9 multiply_bitcast_fusion.1
  86.6 1.1 %copy.309 = f32[5,12,256]{1,2,0:T(8,128)} copy(f32[5,12,256]{2,1,0:T(8,128)S(1)} %multiply_bitcast_fusion.1) | data formatting | bytes 122880 | tf_op jit(solution)/shard_map/mul | solution.py:141
  87.7 1.5 %broadcast_in_dim.21 = f32[5,12,256,4]{1,3,2,0:T(4,128)S(1)} broadcast(f32[5,12,256]{1,2,0:T(8,128)} %copy.309), dimensions={0,1,2} | broadcast | bytes 307200 | tf_op jit(solution)/shard_map/broadcast_in_dim | solution.py:85
  89.3 1.5 %copy.310 = f32[1,5,12,1024]{3,2,1,0:T(8,128)} copy(f32[1,5,12,1024]{2,3,1,0:T(8,128)S(1)} %bitcast.469) | data formatting | bytes 491520 | tf_op jit(solution)/shard_map/broadcast_in_dim | solution.py:85
  91.0 1.9 %fusion.4 = f32[1,5,12,1024]{3,2,1,0:T(8,128)S(1)} fusion(f32[1,5,24,1024]{3,0,1,2:T(1,128)S(1)} %all_gather.18, f32[1,5,12,1024]{3,2,1,0:T(8,128)} %copy.317, f32[1,5,12,1024]{3,2,1,0:T(8,128)} %copy.310, f32[1,5,12,1024]{3,2,1,0:T(8,128)} %copy-done.5, f32[1,5,12,1023]{3,2,1,0:T(8,128)S(1)} %bitcast.465, f32[1024]{0:T(1024)S(1)} %get-tuple-element.89, ...), kind=kOutput, calls=%fused_computation.6 | convolution fusion | flops 18186528 | bytes 1987476 | tf_op jit(solution)/shard_map/ts,pvsc->pvtc/dot_general | solution.py:67
  92.9 1.0 fusion.45
  94.3 0.9 copy.372
  95.2 2.0 %copy.370 = f32[5,12,256]{1,2,0:T(8,128)} copy(f32[5,12,256]{2,1,0:T(8,128)} %bitcast.136) | data formatting | bytes 122880 | tf_op jit(solution)/shard_map/ppermute | solution.py:14
  97.3 1.5 %broadcast_in_dim.52 = f32[5,12,256,4]{1,3,2,0:T(4,128)S(1)} broadcast(f32[5,12,256]{1,2,0:T(8,128)} %copy.370), dimensions={0,1,2} | broadcast | bytes 307200 | tf_op jit(solution)/shard_map/broadcast_in_dim | solution.py:85
  98.8 1.5 %copy.371 = f32[1,5,12,1024]{3,2,1,0:T(8,128)} copy(f32[1,5,12,1024]{2,3,1,0:T(8,128)S(1)} %bitcast.470) | data formatting | bytes 491520 | tf_op jit(solution)/shard_map/broadcast_in_dim | solution.py:85
  100.3 2.0 %copy.364 = f32[5,12,256]{1,2,0:T(8,128)} copy(f32[5,12,256]{2,1,0:T(8,128)} %bitcast.132) | data formatting | bytes 122880 | tf_op jit(solution)/shard_map/ppermute | solution.py:14
  102.3 1.6 %broadcast_in_dim.50 = f32[5,12,256,4]{1,3,2,0:T(4,128)S(1)} broadcast(f32[5,12,256]{1,2,0:T(8,128)} %copy.364), dimensions={0,1,2} | broadcast | bytes 307200 | tf_op jit(solution)/shard_map/broadcast_in_dim | solution.py:85
  104.0 1.5 %copy.365 = f32[1,5,12,1024]{3,2,1,0:T(8,128)} copy(f32[1,5,12,1024]{2,3,1,0:T(8,128)S(1)} %bitcast.471) | data formatting | bytes 491520 | tf_op jit(solution)/shard_map/broadcast_in_dim | solution.py:85
  105.5 1.7 %fusion.7 = f32[1,5,12,1024]{3,2,1,0:T(8,128)S(1)} fusion(f32[1,5,24,1024]{3,0,1,2:T(1,128)S(1)} %copy-done, f32[1,5,12,1024]{3,2,1,0:T(8,128)} %copy.371, f32[1,5,12,1024]{3,2,1,0:T(8,128)} %copy.365, f32[1,5,12,1024]{3,2,1,0:T(8,128)} %copy-done.4, f32[1,5,12,1023]{3,2,1,0:T(8,128)S(1)} %copy-done.2, f32[1024]{0:T(1024)S(1)} %get-tuple-element.89, ...), kind=kOutput, calls=%fused_computation.9 | convolution fusion | flops 18125088 | bytes 1826820 | tf_op jit(solution)/shard_map/ts,pvsc->pvtc/dot_general | solution.py:67
  107.2 0.9 copy.373
  (203 shorter events, 11.5 us)
Async XLA Ops:
  6.0 12.8 %copy-start.70 = (s32[11]{0:T(128)S(1)}, s32[11]{0:T(128)}, u32[]{:S(2)}) copy-start(s32[11]{0:T(128)} %param.19) | copy-start | bytes 136
  21.5 59.1 %collective-permute-start.1 = (f32[1,5,12,256]{3,2,1,0:T(8,128)}, f32[1,5,12,256]{3,2,1,0:T(8,128)}, u32[]{:S(2)}, u32[]{:S(2)}) collective-permute-start(f32[1,5,12,256]{3,2,1,0:T(8,128)} %convolution_bitcast_fusion.2), channel_id=1, source_target_pairs={{510,0},{0,2},{2,4},{4,6},{6,8},{8,10},{10,12},{12,14},{14,16},{16... | collective-permute-start | bytes 184328 | tf_op jit(solution)/shard_map/ppermute | solution.py:14
  27.0 21.8 %copy-start.1 = (bf16[1,12,25,1024]{3,2,1,0:T(8,128)(2,1)S(1)}, bf16[1,12,25,1024]{3,2,1,0:T(8,128)(2,1)}, u32[]{:S(2)}) copy-start(bf16[1,12,25,1024]{3,2,1,0:T(8,128)(2,1)} %param.13) | copy-start | bytes 1843204
  31.4 19.2 %copy-start.63 = (f32[1,5,12,1024]{3,0,2,1:T(1,128)S(1)}, f32[1,5,12,1024]{3,0,2,1:T(1,128)}, u32[]{:S(2)}) copy-start(f32[1,5,12,1024]{3,0,2,1:T(1,128)} %param.11) | copy-start | bytes 737284
  31.4 54.3 %collective-permute-start = (f32[1,5,12,256]{3,2,1,0:T(8,128)}, f32[1,5,12,256]{3,2,1,0:T(8,128)}, u32[]{:S(2)}, u32[]{:S(2)}) collective-permute-start(f32[1,5,12,256]{3,2,1,0:T(8,128)} %convolution_bitcast_fusion.3), channel_id=1, source_target_pairs={{2,0},{4,2},{6,4},{8,6},{10,8},{12,10},{14,12},{16,14},{18,16},{20... | collective-permute-start | bytes 184328 | tf_op jit(solution)/shard_map/ppermute | solution.py:14
  50.2 2.9 %copy-start.12 = (bf16[1,12,1,1024]{3,2,1,0:T(2,128)(2,1)}, bf16[1,12,1,1024]{3,2,1,0:T(2,128)(2,1)S(1)}, u32[]{:S(2)}) copy-start(bf16[1,12,1,1024]{3,2,1,0:T(2,128)(2,1)S(1)} %get-tuple-element.20) | copy-start | bytes 73732
  53.3 4.4 %copy-start.67 = (f32[1,256]{1,0:T(1,128)S(1)}, f32[1,256]{1,0:T(1,128)}, u32[]{:S(2)}) copy-start(f32[1,256]{1,0:T(1,128)} %param.16) | copy-start | bytes 3076
  53.5 11.1 %copy-start.69 = (f32[1,256]{1,0:T(1,128)S(1)}, f32[1,256]{1,0:T(1,128)}, u32[]{:S(2)}) copy-start(f32[1,256]{1,0:T(1,128)} %param.15) | copy-start | bytes 3076
  53.5 14.1 %copy-start.3 = (f32[1,5,12,1024]{3,0,2,1:T(1,128)S(1)}, f32[1,5,12,1024]{3,0,2,1:T(1,128)}, u32[]{:S(2)}) copy-start(f32[1,5,12,1024]{3,0,2,1:T(1,128)} %param.10) | copy-start | bytes 737284
  54.4 16.9 %copy-start.50 = (bf16[1,12,1,1024]{3,2,1,0:T(2,128)(2,1)S(1)}, bf16[1,12,1,1024]{3,2,1,0:T(2,128)(2,1)}, u32[]{:S(2)}) copy-start(bf16[1,12,1,1024]{3,2,1,0:T(2,128)(2,1)} %get-tuple-element.60) | copy-start | bytes 73732
  54.4 16.9 %copy-start.54 = (bf16[1,12,1,1024]{3,2,1,0:T(2,128)(2,1)S(1)}, bf16[1,12,1,1024]{3,2,1,0:T(2,128)(2,1)}, u32[]{:S(2)}) copy-start(bf16[1,12,1,1024]{3,2,1,0:T(2,128)(2,1)} %get-tuple-element.61) | copy-start | bytes 73732
  54.6 17.6 %copy-start.49 = (bf16[1,12,1,1024]{3,2,1,0:T(2,128)(2,1)S(1)}, bf16[1,12,1,1024]{3,2,1,0:T(2,128)(2,1)}, u32[]{:S(2)}) copy-start(bf16[1,12,1,1024]{3,2,1,0:T(2,128)(2,1)} %get-tuple-element.55) | copy-start | bytes 73732
  54.6 17.6 %copy-start.53 = (bf16[1,12,1,1024]{3,2,1,0:T(2,128)(2,1)S(1)}, bf16[1,12,1,1024]{3,2,1,0:T(2,128)(2,1)}, u32[]{:S(2)}) copy-start(bf16[1,12,1,1024]{3,2,1,0:T(2,128)(2,1)} %get-tuple-element.56) | copy-start | bytes 73732
  54.7 17.6 %copy-start.60 = (bf16[1,12,1,1024]{3,2,1,0:T(2,128)(2,1)S(1)}, bf16[1,12,1,1024]{3,2,1,0:T(2,128)(2,1)}, u32[]{:S(2)}) copy-start(bf16[1,12,1,1024]{3,2,1,0:T(2,128)(2,1)} %get-tuple-element.57) | copy-start | bytes 73732
  54.9 18.2 %copy-start.56 = (bf16[1,12,1,1024]{3,2,1,0:T(2,128)(2,1)S(1)}, bf16[1,12,1,1024]{3,2,1,0:T(2,128)(2,1)}, u32[]{:S(2)}) copy-start(bf16[1,12,1,1024]{3,2,1,0:T(2,128)(2,1)} %get-tuple-element.48) | copy-start | bytes 73732
  55.3 18.7 %copy-start.48 = (bf16[1,12,1,1024]{3,2,1,0:T(2,128)(2,1)S(1)}, bf16[1,12,1,1024]{3,2,1,0:T(2,128)(2,1)}, u32[]{:S(2)}) copy-start(bf16[1,12,1,1024]{3,2,1,0:T(2,128)(2,1)} %get-tuple-element.50) | copy-start | bytes 73732
  55.3 18.7 %copy-start.52 = (bf16[1,12,1,1024]{3,2,1,0:T(2,128)(2,1)S(1)}, bf16[1,12,1,1024]{3,2,1,0:T(2,128)(2,1)}, u32[]{:S(2)}) copy-start(bf16[1,12,1,1024]{3,2,1,0:T(2,128)(2,1)} %get-tuple-element.51) | copy-start | bytes 73732
  55.3 18.7 %copy-start.59 = (bf16[1,12,1,1024]{3,2,1,0:T(2,128)(2,1)S(1)}, bf16[1,12,1,1024]{3,2,1,0:T(2,128)(2,1)}, u32[]{:S(2)}) copy-start(bf16[1,12,1,1024]{3,2,1,0:T(2,128)(2,1)} %get-tuple-element.52) | copy-start | bytes 73732
  58.6 36.7 %collective-permute-start.3 = (f32[1,5,12,256]{3,2,1,0:T(8,128)}, f32[1,5,12,256]{3,2,1,0:T(8,128)}, u32[]{:S(2)}, u32[]{:S(2)}) collective-permute-start(f32[1,5,12,256]{3,2,1,0:T(8,128)} %fusion.11), channel_id=1, source_target_pairs={{2,0},{4,2},{6,4},{8,6},{10,8},{12,10},{14,12},{16,14},{18,16},{20... | collective-permute-start | bytes 184328 | tf_op jit(solution)/shard_map/ppermute | solution.py:14
  62.3 12.7 %copy-start.55 = (bf16[1,12,1,1024]{3,2,1,0:T(2,128)(2,1)S(1)}, bf16[1,12,1,1024]{3,2,1,0:T(2,128)(2,1)}, u32[]{:S(2)}) copy-start(bf16[1,12,1,1024]{3,2,1,0:T(2,128)(2,1)} %get-tuple-element.47) | copy-start | bytes 73732
  65.6 10.3 %copy-start.47 = (bf16[1,12,1,1024]{3,2,1,0:T(2,128)(2,1)S(1)}, bf16[1,12,1,1024]{3,2,1,0:T(2,128)(2,1)}, u32[]{:S(2)}) copy-start(bf16[1,12,1,1024]{3,2,1,0:T(2,128)(2,1)} %get-tuple-element.45) | copy-start | bytes 73732
  65.6 10.3 %copy-start.51 = (bf16[1,12,1,1024]{3,2,1,0:T(2,128)(2,1)S(1)}, bf16[1,12,1,1024]{3,2,1,0:T(2,128)(2,1)}, u32[]{:S(2)}) copy-start(bf16[1,12,1,1024]{3,2,1,0:T(2,128)(2,1)} %get-tuple-element.46) | copy-start | bytes 73732
  65.6 10.3 %copy-start.58 = (bf16[1,12,1,1024]{3,2,1,0:T(2,128)(2,1)S(1)}, bf16[1,12,1,1024]{3,2,1,0:T(2,128)(2,1)}, u32[]{:S(2)}) copy-start(bf16[1,12,1,1024]{3,2,1,0:T(2,128)(2,1)} %copy-done.57) | copy-start | bytes 73732
  65.6 34.7 %collective-permute-start.2 = (f32[1,5,12,256]{3,2,1,0:T(8,128)}, f32[1,5,12,256]{3,2,1,0:T(8,128)}, u32[]{:S(2)}, u32[]{:S(2)}) collective-permute-start(f32[1,5,12,256]{3,2,1,0:T(8,128)} %fusion.9), channel_id=1, source_target_pairs={{510,0},{0,2},{2,4},{4,6},{6,8},{8,10},{10,12},{12,14},{14,16},{16... | collective-permute-start | bytes 184328 | tf_op jit(solution)/shard_map/ppermute | solution.py:14
  74.1 5.4 %copy-start.66 = (f32[1,1024]{1,0:T(1,128)S(1)}, f32[1,1024]{1,0:T(1,128)}, u32[]{:S(2)}) copy-start(f32[1,1024]{1,0:T(1,128)} %param.14) | copy-start | bytes 12292
  75.0 5.6 %copy-start.68 = (f32[1,256]{1,0:T(1,128)S(1)}, f32[1,256]{1,0:T(1,128)}, u32[]{:S(2)}) copy-start(f32[1,256]{1,0:T(1,128)} %param.16) | copy-start | bytes 3076
  76.7 4.8 %copy-start.4 = (f32[1,5,12,1024]{3,2,1,0:T(8,128)}, f32[1,5,12,1024]{3,2,1,0:T(8,128)S(1)}, u32[]{:S(2)}) copy-start(f32[1,5,12,1024]{3,2,1,0:T(8,128)S(1)} %get-tuple-element.78) | copy-start | bytes 737284
  90.8 3.0 %copy-start.9 = (bf16[1,12,1,1024]{3,2,1,0:T(2,128)(2,1)S(1)}, bf16[1,12,1,1024]{3,2,1,0:T(2,128)(2,1)}, u32[]{:S(2)}) copy-start(bf16[1,12,1,1024]{3,2,1,0:T(2,128)(2,1)} %copy-done.8) | copy-start | bytes 73732
  90.8 3.1 %copy-start.37 = (bf16[1,12,1,1024]{3,2,1,0:T(2,128)(2,1)S(1)}, bf16[1,12,1,1024]{3,2,1,0:T(2,128)(2,1)}, u32[]{:S(2)}) copy-start(bf16[1,12,1,1024]{3,2,1,0:T(2,128)(2,1)} %copy-done.36) | copy-start | bytes 73732
  90.8 3.1 %copy-start.39 = (bf16[1,12,1,1024]{3,2,1,0:T(2,128)(2,1)S(1)}, bf16[1,12,1,1024]{3,2,1,0:T(2,128)(2,1)}, u32[]{:S(2)}) copy-start(bf16[1,12,1,1024]{3,2,1,0:T(2,128)(2,1)} %copy-done.38) | copy-start | bytes 73732
  90.8 3.1 %copy-start.41 = (bf16[1,12,1,1024]{3,2,1,0:T(2,128)(2,1)S(1)}, bf16[1,12,1,1024]{3,2,1,0:T(2,128)(2,1)}, u32[]{:S(2)}) copy-start(bf16[1,12,1,1024]{3,2,1,0:T(2,128)(2,1)} %copy-done.40) | copy-start | bytes 73732
  90.8 3.1 %copy-start.43 = (bf16[1,12,1,1024]{3,2,1,0:T(2,128)(2,1)S(1)}, bf16[1,12,1,1024]{3,2,1,0:T(2,128)(2,1)}, u32[]{:S(2)}) copy-start(bf16[1,12,1,1024]{3,2,1,0:T(2,128)(2,1)} %copy-done.42) | copy-start | bytes 73732
  90.8 3.1 %copy-start.7 = (bf16[1,12,1,1024]{3,2,1,0:T(2,128)(2,1)S(1)}, bf16[1,12,1,1024]{3,2,1,0:T(2,128)(2,1)}, u32[]{:S(2)}) copy-start(bf16[1,12,1,1024]{3,2,1,0:T(2,128)(2,1)} %copy-done.6) | copy-start | bytes 73732
  90.8 3.1 %copy-start.29 = (bf16[1,12,1,1024]{3,2,1,0:T(2,128)(2,1)S(1)}, bf16[1,12,1,1024]{3,2,1,0:T(2,128)(2,1)}, u32[]{:S(2)}) copy-start(bf16[1,12,1,1024]{3,2,1,0:T(2,128)(2,1)} %copy-done.28) | copy-start | bytes 73732
  90.8 3.1 %copy-start.31 = (bf16[1,12,1,1024]{3,2,1,0:T(2,128)(2,1)S(1)}, bf16[1,12,1,1024]{3,2,1,0:T(2,128)(2,1)}, u32[]{:S(2)}) copy-start(bf16[1,12,1,1024]{3,2,1,0:T(2,128)(2,1)} %copy-done.30) | copy-start | bytes 73732
  90.8 3.1 %copy-start.33 = (bf16[1,12,1,1024]{3,2,1,0:T(2,128)(2,1)S(1)}, bf16[1,12,1,1024]{3,2,1,0:T(2,128)(2,1)}, u32[]{:S(2)}) copy-start(bf16[1,12,1,1024]{3,2,1,0:T(2,128)(2,1)} %copy-done.32) | copy-start | bytes 73732
  90.9 3.1 %copy-start.35 = (bf16[1,12,1,1024]{3,2,1,0:T(2,128)(2,1)S(1)}, bf16[1,12,1,1024]{3,2,1,0:T(2,128)(2,1)}, u32[]{:S(2)}) copy-start(bf16[1,12,1,1024]{3,2,1,0:T(2,128)(2,1)} %copy-done.34) | copy-start | bytes 73732
  90.9 3.2 %copy-start.21 = (bf16[1,12,1,1024]{3,2,1,0:T(2,128)(2,1)S(1)}, bf16[1,12,1,1024]{3,2,1,0:T(2,128)(2,1)}, u32[]{:S(2)}) copy-start(bf16[1,12,1,1024]{3,2,1,0:T(2,128)(2,1)} %copy-done.20) | copy-start | bytes 73732
  90.9 3.2 %copy-start.23 = (bf16[1,12,1,1024]{3,2,1,0:T(2,128)(2,1)S(1)}, bf16[1,12,1,1024]{3,2,1,0:T(2,128)(2,1)}, u32[]{:S(2)}) copy-start(bf16[1,12,1,1024]{3,2,1,0:T(2,128)(2,1)} %copy-done.22) | copy-start | bytes 73732
  90.9 3.2 %copy-start.25 = (bf16[1,12,1,1024]{3,2,1,0:T(2,128)(2,1)S(1)}, bf16[1,12,1,1024]{3,2,1,0:T(2,128)(2,1)}, u32[]{:S(2)}) copy-start(bf16[1,12,1,1024]{3,2,1,0:T(2,128)(2,1)} %copy-done.24) | copy-start | bytes 73732
  90.9 3.2 %copy-start.27 = (bf16[1,12,1,1024]{3,2,1,0:T(2,128)(2,1)S(1)}, bf16[1,12,1,1024]{3,2,1,0:T(2,128)(2,1)}, u32[]{:S(2)}) copy-start(bf16[1,12,1,1024]{3,2,1,0:T(2,128)(2,1)} %copy-done.26) | copy-start | bytes 73732
  90.9 3.3 %copy-start.13 = (bf16[1,12,1,1024]{3,2,1,0:T(2,128)(2,1)S(1)}, bf16[1,12,1,1024]{3,2,1,0:T(2,128)(2,1)}, u32[]{:S(2)}) copy-start(bf16[1,12,1,1024]{3,2,1,0:T(2,128)(2,1)} %copy-done.12) | copy-start | bytes 73732
  90.9 3.3 %copy-start.15 = (bf16[1,12,1,1024]{3,2,1,0:T(2,128)(2,1)S(1)}, bf16[1,12,1,1024]{3,2,1,0:T(2,128)(2,1)}, u32[]{:S(2)}) copy-start(bf16[1,12,1,1024]{3,2,1,0:T(2,128)(2,1)} %copy-done.14) | copy-start | bytes 73732
  90.9 3.3 %copy-start.17 = (bf16[1,12,1,1024]{3,2,1,0:T(2,128)(2,1)S(1)}, bf16[1,12,1,1024]{3,2,1,0:T(2,128)(2,1)}, u32[]{:S(2)}) copy-start(bf16[1,12,1,1024]{3,2,1,0:T(2,128)(2,1)} %copy-done.16) | copy-start | bytes 73732
  90.9 3.3 %copy-start.19 = (bf16[1,12,1,1024]{3,2,1,0:T(2,128)(2,1)S(1)}, bf16[1,12,1,1024]{3,2,1,0:T(2,128)(2,1)}, u32[]{:S(2)}) copy-start(bf16[1,12,1,1024]{3,2,1,0:T(2,128)(2,1)} %copy-done.18) | copy-start | bytes 73732
  102.3 3.1 %copy-start = (f32[1,5,24,1024]{3,0,1,2:T(1,128)S(1)}, f32[1,5,24,1024]{3,0,1,2:T(1,128)}, u32[]{:S(2)}) copy-start(f32[1,5,24,1024]{3,0,1,2:T(1,128)} %all_gather.21) | copy-start | bytes 1474564
  102.3 3.1 %copy-start.2 = (f32[1,5,12,1023]{3,2,1,0:T(8,128)S(1)}, f32[1,5,12,1023]{3,2,1,0:T(8,128)}, u32[]{:S(2)}) copy-start(f32[1,5,12,1023]{3,2,1,0:T(8,128)} %slice_multiply_fusion) | copy-start | bytes 736564
  102.3 3.1 %copy-start.65 = (f32[24,24]{1,0:T(8,128)S(1)}, f32[24,24]{1,0:T(8,128)}, u32[]{:S(2)}) copy-start(f32[24,24]{1,0:T(8,128)} %get-tuple-element.86) | copy-start | bytes 6916
  (27 other events, 72.7 us)
where the time goes:
time: 110 us; the launch traced here: 108 us
  local copies, waits for them, and re-layouts  39.6 us (36%)
  other arithmetic  21.2 us (19%)
  blocking collectives  19.8 us (18%)
  starting transfers between devices  18.3 us (17%)
  matrix products  7.35 us (7%)
  between operations  1.95 us (2%)
    ppermute x4, starting transfers between devices, passed_along(): return lax.ppermute(block, axis, route)  18.3 us
    broadcast_in_dim x8, local copies, waits for them, and re-layouts, face_spread(): return jnp.repeat(values, 4, axis=-1) * mask  12.2 us
    all_gather x2, blocking collectives, regroup(): lax.all_gather(up_face, 'inst', axis=2, tiled=True)  10.8 us
    unnamed x13, other arithmetic  8.42 us
    dot_general x6, matrix products, instance_mix(): jnp.einsum('ts,pvsc->pvtc', matrix, vector, precision=lax.Precision.HIGHEST)  7.35 us
    reduce_sum x3, other arithmetic, face_pick(): return jnp.sum(picked, axis=-1)  6.04 us
    slice x2, local copies, waits for them, and re-layouts, block_apply(): blocks[:, :, row_index * variables + column_index, :]  5.68 us
    all_gather x2, blocking collectives, regroup(): lax.all_gather(vector, 'inst', axis=2, tiled=True)  4.67 us
  transfers between devices with their start and end apart: 4, of which 0 were waited for; matrix products, arithmetic and copies ran while one was open for 44% of the time, Pallas kernels for 0%

commit v1 on v0

--- a/solution.py
+++ b/solution.py
@@ -95,7 +95,12 @@
     own_rot_t = lax.dynamic_slice_in_dim(rotation.T, first_row, own_count, 0)
     return (
         instance_mix(own_deriv, lax.all_gather(vector, "inst", axis=2, tiled=True)),
-        instance_mix(own_rot, lax.all_gather(lo_face, "inst", axis=2, tiled=True)),
+        instance_mix(
+            own_rot,
+            jnp.concatenate(
+                lax.all_to_all(jnp.stack([lo_face] * lax.axis_size("inst")), "inst", 0, 0), axis=2
+            ),
+        ),
         instance_mix(own_rot_t, lax.all_gather(up_face, "inst", axis=2, tiled=True)),
     )
 

time: 110 us -> 104 us (0.945); the launches traced: 108 us -> 103 us
  local copies, waits for them, and re-layouts: 39.6 us -> 34.2 us
  blocking collectives: 19.8 us -> 23.6 us
  other arithmetic: 21.2 us -> 17.8 us
    all_to_all x0 -> x2, blocking collectives: none -> 7.94 us  [regroup(): lax.all_to_all(jnp.stack([lo_face] * lax.axis_size('inst')), 'inst', 0, 0)]
    unnamed x13, other arithmetic: 8.42 us -> 3.55 us
    all_gather x2 -> x0, blocking collectives: 4.31 us -> none  [regroup(): lax.all_gather(lo_face, 'inst', axis=2, tiled=True)]
    slice x2, local copies, waits for them, and re-layouts: 5.68 us -> 2.67 us  [block_apply(): blocks[:, :, row_index * variables + column_index, :]]
    reduce_sum x4 -> x2, local copies, waits for them, and re-layouts: 3 us -> 1.46 us  [face_pick(): return jnp.sum(picked, axis=-1)]
    another operation x0 -> x2, other arithmetic: none -> 1.49 us  [regroup(): jnp.stack([lo_face] * lax.axis_size('inst'))]
    slice x2, local copies, waits for them, and re-layouts: 2.33 us -> 1.16 us  [block_apply(): summed = blocks[:, :, row_index * variables, :] * vector[:, 0]]
    unnamed x151 -> x194, local copies, waits for them, and re-layouts: 2.94 us -> 3.97 us
  transfers between devices with their start and end apart: 4 -> 4, of which waited for: 0 -> 0; matrix products, arithmetic and copies ran while one was open for 44% -> 37% of each run, Pallas kernels for 0% -> 0%
where the time goes in v1:
time: 104 us; the launch traced here: 103 us
  local copies, waits for them, and re-layouts  34.2 us (33%)
  blocking collectives  23.6 us (23%)
  starting transfers between devices  18.2 us (18%)
  other arithmetic  17.8 us (17%)
  matrix products  7.29 us (7%)
  between operations  2.23 us (2%)
    ppermute x4, starting transfers between devices, passed_along(): return lax.ppermute(block, axis, route)  18.2 us
    broadcast_in_dim x8, local copies, waits for them, and re-layouts, face_spread(): return jnp.repeat(values, 4, axis=-1) * mask  12.1 us
    all_gather x2, blocking collectives, regroup(): lax.all_gather(up_face, 'inst', axis=2, tiled=True)  10.8 us
    all_to_all x2, blocking collectives, regroup(): lax.all_to_all(jnp.stack([lo_face] * lax.axis_size('inst')), 'inst', 0, 0)  7.94 us
    dot_general x6, matrix products, instance_mix(): jnp.einsum('ts,pvsc->pvtc', matrix, vector, precision=lax.Precision.HIGHEST)  7.29 us
    reduce_sum x3, other arithmetic, face_pick(): return jnp.sum(picked, axis=-1)  6 us
    all_gather x2, blocking collectives, regroup(): lax.all_gather(vector, 'inst', axis=2, tiled=True)  4.79 us
    ppermute x2, local copies, waits for them, and re-layouts, passed_along(): return lax.ppermute(block, axis, route)  4 us
  transfers between devices with their start and end apart: 4, of which 0 were waited for; matrix products, arithmetic and copies ran while one was open for 37% of the time, Pallas kernels for 0%

profile of v1, /device:TPU:1, one launch (start us, length us, event | category | flops | bytes accessed | tf_op | source)
XLA Modules:
  0.0 103.3 jit_solution(16436088580404145989)
XLA Ops:
  0.7 0.7 fusion.149
  1.6 0.7 fusion.148
  2.5 1.8 %fusion.168 = (f32[1,5,12,1024]{3,2,1,0:T(8,128)S(1)}, f32[1,5,12,1024]{3,2,1,0:T(8,128)S(1)}, f32[1,5,12,1024]{3,2,1,0:T(8,128)}) fusion(f32[1,5,12,1024]{3,0,2,1:T(1,128)} %param.10, f32[1024]{0:T(1024)S(1)} %get-tuple-element.90, f32[1024]{0:T(1024)S(1)} %get-tuple-element.91), kind=kLoop, calls=%fused_computation.354 | loop fusion | flops 122880 | bytes 991232 | tf_op args[0]
  4.3 1.7 %copy.420 = f32[1,5,12,1024]{2,3,1,0:T(8,128)S(1)} copy(f32[1,5,12,1024]{3,2,1,0:T(8,128)} %get-tuple-element.79) | data formatting | bytes 491520 | tf_op jit(solution)/shard_map/mul | solution.py:80
  6.0 2.8 %reduce_sum.61 = f32[5,12,256]{1,2,0:T(8,128)} reduce(f32[5,12,256,4]{1,3,2,0:T(4,128)S(1)} %bitcast.473, f32[]{:T(128)} %constant.66.clone.1), dimensions={3}, to_apply=%region_3.4 | reduce | flops 46080 | bytes 307204 | tf_op jit(solution)/shard_map/reduce_sum | solution.py:81
  8.8 1.4 %copy.421 = f32[5,12,256]{2,0,1:T(8,128)S(1)} copy(f32[5,12,256]{1,2,0:T(8,128)} %reduce_sum.61) | data formatting | bytes 122880 | tf_op jit(solution)/shard_map/reduce_sum | solution.py:81
  10.3 8.5 %all-gather = f32[5,24,256]{2,0,1:T(8,128)S(1)} all-gather(f32[5,12,256]{2,0,1:T(8,128)S(1)} %copy.421), channel_id=2, replica_groups=mesh['blade'=256,'inst'=2] {'inst'}, dimensions={1}, use_global_device_ids=true | all-gather | bytes 184320 | tf_op jit(solution)/shard_map/all_gather | solution.py:104
  18.8 1.6 %multiply_reduce_fusion.2 = (f32[24,24]{1,0:T(8,128)}, f32[24,24]{1,0:T(8,128)S(1)}) fusion(s32[24,24]{1,0:T(8,128)S(1)} %iota_subtract_fusion, s32[11]{0:T(128)S(1)} %get-tuple-element.92, f32[11]{0:T(128)S(1)} %get-tuple-element.93, f32[11]{0:T(128)S(1)} %convert_multiply_fusion.75), kind=kLoop, calls=%fused_computation.33 | loop fusion | flops 93888 | bytes 7044 | tf_op jit(solution)/shard_map/reduce_sum | solution.py:28
  20.4 1.0 convolution_bitcast_fusion.2
  21.4 1.9 %collective-permute-start.1 = (f32[1,5,12,256]{3,2,1,0:T(8,128)}, f32[1,5,12,256]{3,2,1,0:T(8,128)}, u32[]{:S(2)}, u32[]{:S(2)}) collective-permute-start(f32[1,5,12,256]{3,2,1,0:T(8,128)} %convolution_bitcast_fusion.2), channel_id=1, source_target_pairs={{510,0},{0,2},{2,4},{4,6},{6,8},{8,10},{10,12},{12,14},{14,16},{16... | collective-permute-start | bytes 184328 | tf_op jit(solution)/shard_map/ppermute | solution.py:14
  23.3 0.8 copy.414
  24.1 2.8 %reduce_sum.59 = f32[5,12,256]{1,2,0:T(8,128)} reduce(f32[5,12,256,4]{1,3,2,0:T(4,128)S(1)} %bitcast.472, f32[]{:T(128)} %constant.66.clone.1), dimensions={3}, to_apply=%region_1.2 | reduce | flops 46080 | bytes 307204 | tf_op jit(solution)/shard_map/reduce_sum | solution.py:81
  27.0 1.4 %pad_maximum_fusion = f32[2,1,5,12,256]{3,4,2,1,0:T(8,128)S(1)} fusion(f32[1,1,5,12,256]{3,4,2,1,0:T(8,128)} %bitcast.479), kind=kLoop, calls=%fused_computation | loop fusion | flops 30720 | bytes 184320 | tf_op jit(solution)/shard_map/stack | solution.py:101
  28.8 3.8 %all_to_all.10 = f32[2,1,5,12,256]{4,1,3,2,0:T(1,128)S(1)} all-to-all(f32[2,1,5,12,256]{4,1,3,2,0:T(1,128)S(1)} %copy.415), channel_id=1, replica_groups=mesh['blade'=256,'inst'=2] {'inst'}, dimensions={0} | all-to-all | bytes 245760 | tf_op jit(solution)/shard_map/all_to_all | solution.py:101
  32.7 0.8 convolution_bitcast_fusion.3
  33.5 10.6 %collective-permute-start = (f32[1,5,12,256]{3,2,1,0:T(8,128)}, f32[1,5,12,256]{3,2,1,0:T(8,128)}, u32[]{:S(2)}, u32[]{:S(2)}) collective-permute-start(f32[1,5,12,256]{3,2,1,0:T(8,128)} %convolution_bitcast_fusion.3), channel_id=1, source_target_pairs={{2,0},{4,2},{6,4},{8,6},{10,8},{12,10},{14,12},{16,14},{18,16},{20... | collective-permute-start | bytes 184328 | tf_op jit(solution)/shard_map/ppermute | solution.py:14
  44.1 0.9 fusion.166
  45.0 1.7 %fusion.165 = (bf16[1,12,1,1024]{3,2,1,0:T(2,128)(2,1)}, bf16[1,12,1,1024]{3,2,1,0:T(2,128)(2,1)}, bf16[1,12,1,1024]{3,2,1,0:T(2,128)(2,1)}, bf16[1,12,1,1024]{3...) fusion(bf16[1,12,25,1024]{3,2,1,0:T(8,128)(2,1)S(1)} %copy-done.1), kind=kLoop, calls=%fused_computation.351 | loop fusion | bytes 933888 | tf_op jit(solution)/shard_map/slice | solution.py:46
  47.0 1.0 fusion.163
  48.5 1.1 %fusion.38 = (f32[1,5,12,1024]{3,2,1,0:T(8,128)}, f32[1,1,12,1024]{3,2,1,0:T(8,128)S(1)}, f32[1,1,12,1024]{3,2,1,0:T(8,128)S(1)}, f32[1,1,12,1024]{3,2,1,0:T(8,1...) fusion(bf16[1,12,1,1024]{3,2,1,0:T(2,128)(2,1)S(1)} %get-tuple-element.71, ...), kind=kLoop, calls=%fused_computation.159 | loop fusion | flops 1032191 | bytes 1294336
  53.4 4.1 %all_to_all.11 = f32[2,1,5,12,256]{4,1,3,2,0:T(1,128)S(1)} all-to-all(f32[2,1,5,12,256]{4,1,3,2,0:T(1,128)S(1)} %copy.476), channel_id=1, replica_groups=mesh['blade'=256,'inst'=2] {'inst'}, dimensions={0} | all-to-all | bytes 245760 | tf_op jit(solution)/shard_map/all_to_all | solution.py:101
  57.7 0.8 fusion.11
  58.5 3.6 %collective-permute-start.3 = (f32[1,5,12,256]{3,2,1,0:T(8,128)}, f32[1,5,12,256]{3,2,1,0:T(8,128)}, u32[]{:S(2)}, u32[]{:S(2)}) collective-permute-start(f32[1,5,12,256]{3,2,1,0:T(8,128)} %fusion.11), channel_id=1, source_target_pairs={{2,0},{4,2},{6,4},{8,6},{10,8},{12,10},{14,12},{16,14},{18,16},{20... | collective-permute-start | bytes 184328 | tf_op jit(solution)/shard_map/ppermute | solution.py:14
  62.2 2.4 %all-gather.1 = f32[5,24,256]{2,0,1:T(8,128)S(1)} all-gather(f32[5,12,256]{2,0,1:T(8,128)S(1)} %copy.469), channel_id=3, replica_groups=mesh['blade'=256,'inst'=2] {'inst'}, dimensions={1}, use_global_device_ids=true | all-gather | bytes 184320 | tf_op jit(solution)/shard_map/all_gather | solution.py:104
  64.6 1.0 fusion.9
  65.6 2.1 %collective-permute-start.2 = (f32[1,5,12,256]{3,2,1,0:T(8,128)}, f32[1,5,12,256]{3,2,1,0:T(8,128)}, u32[]{:S(2)}, u32[]{:S(2)}) collective-permute-start(f32[1,5,12,256]{3,2,1,0:T(8,128)} %fusion.9), channel_id=1, source_target_pairs={{510,0},{0,2},{2,4},{4,6},{6,8},{8,10},{10,12},{12,14},{14,16},{16... | collective-permute-start | bytes 184328 | tf_op jit(solution)/shard_map/ppermute | solution.py:14
  67.7 2.3 %all_gather.12 = f32[1,5,24,1024]{3,0,1,2:T(1,128)S(1)} all-gather(f32[1,5,12,1024]{3,0,1,2:T(1,128)S(1)} %copy.411), channel_id=1, replica_groups=mesh['blade'=256,'inst'=2] {'inst'}, dimensions={2}, use_global_device_ids=true | all-gather | bytes 737280 | tf_op jit(solution)/shard_map/all_gather | solution.py:97
  70.1 0.6 fusion.157
  72.7 2.5 %all_gather.14 = f32[1,5,24,1024]{3,0,1,2:T(1,128)} all-gather(f32[1,5,12,1024]{3,0,1,2:T(1,128)S(1)} %copy.455), channel_id=1, replica_groups=mesh['blade'=256,'inst'=2] {'inst'}, dimensions={2}, use_global_device_ids=true | all-gather | bytes 737280 | tf_op jit(solution)/shard_map/all_gather | solution.py:97
  75.2 0.9 slice_multiply_fusion
  76.3 0.9 multiply_bitcast_fusion
  77.2 1.1 %copy.424 = f32[5,12,256]{1,2,0:T(8,128)} copy(f32[5,12,256]{2,1,0:T(8,128)S(1)} %multiply_bitcast_fusion) | data formatting | bytes 122880 | tf_op jit(solution)/shard_map/mul | solution.py:147
  78.3 1.5 %broadcast_in_dim.48 = f32[5,12,256,4]{1,3,2,0:T(4,128)S(1)} broadcast(f32[5,12,256]{1,2,0:T(8,128)} %copy.424), dimensions={0,1,2} | broadcast | bytes 307200 | tf_op jit(solution)/shard_map/broadcast_in_dim | solution.py:85
  79.9 1.5 %copy.425 = f32[1,5,12,1024]{3,2,1,0:T(8,128)} copy(f32[1,5,12,1024]{2,3,1,0:T(8,128)S(1)} %bitcast.474) | data formatting | bytes 491520 | tf_op jit(solution)/shard_map/broadcast_in_dim | solution.py:85
  81.4 0.9 multiply_bitcast_fusion.1
  82.3 1.1 %copy.417 = f32[5,12,256]{1,2,0:T(8,128)} copy(f32[5,12,256]{2,1,0:T(8,128)S(1)} %multiply_bitcast_fusion.1) | data formatting | bytes 122880 | tf_op jit(solution)/shard_map/mul | solution.py:146
  83.4 1.5 %broadcast_in_dim.21 = f32[5,12,256,4]{1,3,2,0:T(4,128)S(1)} broadcast(f32[5,12,256]{1,2,0:T(8,128)} %copy.417), dimensions={0,1,2} | broadcast | bytes 307200 | tf_op jit(solution)/shard_map/broadcast_in_dim | solution.py:85
  84.9 1.5 %copy.418 = f32[1,5,12,1024]{3,2,1,0:T(8,128)} copy(f32[1,5,12,1024]{2,3,1,0:T(8,128)S(1)} %bitcast.475) | data formatting | bytes 491520 | tf_op jit(solution)/shard_map/broadcast_in_dim | solution.py:85
  86.5 1.9 %fusion.4 = f32[1,5,12,1024]{3,2,1,0:T(8,128)S(1)} fusion(f32[1,5,24,1024]{3,0,1,2:T(1,128)S(1)} %all_gather.12, f32[1,5,12,1024]{3,2,1,0:T(8,128)} %copy.425, f32[1,5,12,1024]{3,2,1,0:T(8,128)} %copy.418, f32[1,5,12,1024]{3,2,1,0:T(8,128)} %copy-done.7, f32[1,5,12,1023]{3,2,1,0:T(8,128)S(1)} %bitcast.471, f32[1024]{0:T(1024)S(1)} %get-tuple-element.91, ...), kind=kOutput, calls=%fused_computation.8 | convolution fusion | flops 18186528 | bytes 1987476 | tf_op jit(solution)/shard_map/ts,pvsc->pvtc/dot_general | solution.py:67
  89.5 0.9 copy.480
  90.5 2.0 %copy.478 = f32[5,12,256]{1,2,0:T(8,128)} copy(f32[5,12,256]{2,1,0:T(8,128)} %bitcast.140) | data formatting | bytes 122880 | tf_op jit(solution)/shard_map/ppermute | solution.py:14
  92.5 1.5 %broadcast_in_dim.52 = f32[5,12,256,4]{1,3,2,0:T(4,128)S(1)} broadcast(f32[5,12,256]{1,2,0:T(8,128)} %copy.478), dimensions={0,1,2} | broadcast | bytes 307200 | tf_op jit(solution)/shard_map/broadcast_in_dim | solution.py:85
  94.0 1.5 %copy.479 = f32[1,5,12,1024]{3,2,1,0:T(8,128)} copy(f32[1,5,12,1024]{2,3,1,0:T(8,128)S(1)} %bitcast.476) | data formatting | bytes 491520 | tf_op jit(solution)/shard_map/broadcast_in_dim | solution.py:85
  95.5 2.0 %copy.472 = f32[5,12,256]{1,2,0:T(8,128)} copy(f32[5,12,256]{2,1,0:T(8,128)} %bitcast.134) | data formatting | bytes 122880 | tf_op jit(solution)/shard_map/ppermute | solution.py:14
  97.5 1.5 %broadcast_in_dim.50 = f32[5,12,256,4]{1,3,2,0:T(4,128)S(1)} broadcast(f32[5,12,256]{1,2,0:T(8,128)} %copy.472), dimensions={0,1,2} | broadcast | bytes 307200 | tf_op jit(solution)/shard_map/broadcast_in_dim | solution.py:85
  99.1 1.5 %copy.473 = f32[1,5,12,1024]{3,2,1,0:T(8,128)} copy(f32[1,5,12,1024]{2,3,1,0:T(8,128)S(1)} %bitcast.477) | data formatting | bytes 491520 | tf_op jit(solution)/shard_map/broadcast_in_dim | solution.py:85
  100.6 1.7 %fusion.7 = f32[1,5,12,1024]{3,2,1,0:T(8,128)S(1)} fusion(f32[1,5,24,1024]{3,0,1,2:T(1,128)S(1)} %copy-done, f32[1,5,12,1024]{3,2,1,0:T(8,128)} %copy.479, f32[1,5,12,1024]{3,2,1,0:T(8,128)} %copy.473, f32[1,5,12,1024]{3,2,1,0:T(8,128)} %copy-done.6, f32[1,5,12,1023]{3,2,1,0:T(8,128)S(1)} %copy-done.3, f32[1024]{0:T(1024)S(1)} %get-tuple-element.91, ...), kind=kOutput, calls=%fused_computation.11 | convolution fusion | flops 18125088 | bytes 1826820 | tf_op jit(solution)/shard_map/ts,pvsc->pvtc/dot_general | solution.py:67
  102.3 0.9 copy.481
  (252 shorter events, 8.1 us)
Async XLA Ops:
  6.0 12.8 %copy-start.91 = (s32[11]{0:T(128)S(1)}, s32[11]{0:T(128)}, u32[]{:S(2)}) copy-start(s32[11]{0:T(128)} %param.19) | copy-start | bytes 136
  21.4 54.9 %collective-permute-start.1 = (f32[1,5,12,256]{3,2,1,0:T(8,128)}, f32[1,5,12,256]{3,2,1,0:T(8,128)}, u32[]{:S(2)}, u32[]{:S(2)}) collective-permute-start(f32[1,5,12,256]{3,2,1,0:T(8,128)} %convolution_bitcast_fusion.2), channel_id=1, source_target_pairs={{510,0},{0,2},{2,4},{4,6},{6,8},{8,10},{10,12},{12,14},{14,16},{16... | collective-permute-start | bytes 184328 | tf_op jit(solution)/shard_map/ppermute | solution.py:14
  28.4 15.7 %copy-start.1 = (bf16[1,12,25,1024]{3,2,1,0:T(8,128)(2,1)S(1)}, bf16[1,12,25,1024]{3,2,1,0:T(8,128)(2,1)}, u32[]{:S(2)}) copy-start(bf16[1,12,25,1024]{3,2,1,0:T(8,128)(2,1)} %param.12) | copy-start | bytes 1843204
  32.6 14.0 %copy-start.2 = (bf16[1,12,25,1024]{3,2,1,0:T(8,128)(2,1)S(1)}, bf16[1,12,25,1024]{3,2,1,0:T(8,128)(2,1)}, u32[]{:S(2)}) copy-start(bf16[1,12,25,1024]{3,2,1,0:T(8,128)(2,1)} %param.13) | copy-start | bytes 1843204
  33.5 47.9 %collective-permute-start = (f32[1,5,12,256]{3,2,1,0:T(8,128)}, f32[1,5,12,256]{3,2,1,0:T(8,128)}, u32[]{:S(2)}, u32[]{:S(2)}) collective-permute-start(f32[1,5,12,256]{3,2,1,0:T(8,128)} %convolution_bitcast_fusion.3), channel_id=1, source_target_pairs={{2,0},{4,2},{6,4},{8,6},{10,8},{12,10},{14,12},{16,14},{18,16},{20... | collective-permute-start | bytes 184328 | tf_op jit(solution)/shard_map/ppermute | solution.py:14
  45.0 3.5 %copy-start.20 = (bf16[1,12,1,1024]{3,2,1,0:T(2,128)(2,1)}, bf16[1,12,1,1024]{3,2,1,0:T(2,128)(2,1)S(1)}, u32[]{:S(2)}) copy-start(bf16[1,12,1,1024]{3,2,1,0:T(2,128)(2,1)S(1)} %get-tuple-element.66) | copy-start | bytes 73732
  45.0 3.5 %copy-start.22 = (bf16[1,12,1,1024]{3,2,1,0:T(2,128)(2,1)}, bf16[1,12,1,1024]{3,2,1,0:T(2,128)(2,1)S(1)}, u32[]{:S(2)}) copy-start(bf16[1,12,1,1024]{3,2,1,0:T(2,128)(2,1)S(1)} %get-tuple-element.71) | copy-start | bytes 73732
  53.0 4.7 %copy-start.88 = (f32[1,256]{1,0:T(1,128)S(1)}, f32[1,256]{1,0:T(1,128)}, u32[]{:S(2)}) copy-start(f32[1,256]{1,0:T(1,128)} %param.16) | copy-start | bytes 3076
  53.0 11.6 %copy-start.90 = (f32[1,256]{1,0:T(1,128)S(1)}, f32[1,256]{1,0:T(1,128)}, u32[]{:S(2)}) copy-start(f32[1,256]{1,0:T(1,128)} %param.15) | copy-start | bytes 3076
  53.0 14.6 %copy-start.4 = (f32[1,5,12,1024]{3,0,2,1:T(1,128)S(1)}, f32[1,5,12,1024]{3,0,2,1:T(1,128)}, u32[]{:S(2)}) copy-start(f32[1,5,12,1024]{3,0,2,1:T(1,128)} %param.10) | copy-start | bytes 737284
  57.6 12.5 %copy-start.86 = (f32[24,24]{1,0:T(8,128)S(1)}, f32[24,24]{1,0:T(8,128)}, u32[]{:S(2)}) copy-start(f32[24,24]{1,0:T(8,128)} %get-tuple-element.14) | copy-start | bytes 6916
  57.6 13.1 %copy-start.16 = (bf16[1,12,1,1024]{3,2,1,0:T(2,128)(2,1)S(1)}, bf16[1,12,1,1024]{3,2,1,0:T(2,128)(2,1)}, u32[]{:S(2)}) copy-start(bf16[1,12,1,1024]{3,2,1,0:T(2,128)(2,1)} %get-tuple-element.67) | copy-start | bytes 73732
  57.6 13.1 %copy-start.17 = (bf16[1,12,1,1024]{3,2,1,0:T(2,128)(2,1)S(1)}, bf16[1,12,1,1024]{3,2,1,0:T(2,128)(2,1)}, u32[]{:S(2)}) copy-start(bf16[1,12,1,1024]{3,2,1,0:T(2,128)(2,1)} %get-tuple-element.68) | copy-start | bytes 73732
  57.6 13.1 %copy-start.18 = (bf16[1,12,1,1024]{3,2,1,0:T(2,128)(2,1)S(1)}, bf16[1,12,1,1024]{3,2,1,0:T(2,128)(2,1)}, u32[]{:S(2)}) copy-start(bf16[1,12,1,1024]{3,2,1,0:T(2,128)(2,1)} %get-tuple-element.69) | copy-start | bytes 73732
  57.6 13.1 %copy-start.19 = (bf16[1,12,1,1024]{3,2,1,0:T(2,128)(2,1)S(1)}, bf16[1,12,1,1024]{3,2,1,0:T(2,128)(2,1)}, u32[]{:S(2)}) copy-start(bf16[1,12,1,1024]{3,2,1,0:T(2,128)(2,1)} %get-tuple-element.70) | copy-start | bytes 73732
  57.6 13.1 %copy-start.23 = (bf16[1,12,1,1024]{3,2,1,0:T(2,128)(2,1)S(1)}, bf16[1,12,1,1024]{3,2,1,0:T(2,128)(2,1)}, u32[]{:S(2)}) copy-start(bf16[1,12,1,1024]{3,2,1,0:T(2,128)(2,1)} %copy-done.22) | copy-start | bytes 73732
  58.5 32.0 %collective-permute-start.3 = (f32[1,5,12,256]{3,2,1,0:T(8,128)}, f32[1,5,12,256]{3,2,1,0:T(8,128)}, u32[]{:S(2)}, u32[]{:S(2)}) collective-permute-start(f32[1,5,12,256]{3,2,1,0:T(8,128)} %fusion.11), channel_id=1, source_target_pairs={{2,0},{4,2},{6,4},{8,6},{10,8},{12,10},{14,12},{16,14},{18,16},{20... | collective-permute-start | bytes 184328 | tf_op jit(solution)/shard_map/ppermute | solution.py:14
  62.2 8.7 %copy-start.21 = (bf16[1,12,1,1024]{3,2,1,0:T(2,128)(2,1)S(1)}, bf16[1,12,1,1024]{3,2,1,0:T(2,128)(2,1)}, u32[]{:S(2)}) copy-start(bf16[1,12,1,1024]{3,2,1,0:T(2,128)(2,1)} %copy-done.20) | copy-start | bytes 73732
  62.2 8.7 %copy-start.65 = (bf16[1,12,1,1024]{3,2,1,0:T(2,128)(2,1)S(1)}, bf16[1,12,1,1024]{3,2,1,0:T(2,128)(2,1)}, u32[]{:S(2)}) copy-start(bf16[1,12,1,1024]{3,2,1,0:T(2,128)(2,1)} %get-tuple-element.62) | copy-start | bytes 73732
  62.2 8.7 %copy-start.69 = (bf16[1,12,1,1024]{3,2,1,0:T(2,128)(2,1)S(1)}, bf16[1,12,1,1024]{3,2,1,0:T(2,128)(2,1)}, u32[]{:S(2)}) copy-start(bf16[1,12,1,1024]{3,2,1,0:T(2,128)(2,1)} %get-tuple-element.63) | copy-start | bytes 73732
  62.2 8.7 %copy-start.76 = (bf16[1,12,1,1024]{3,2,1,0:T(2,128)(2,1)S(1)}, bf16[1,12,1,1024]{3,2,1,0:T(2,128)(2,1)}, u32[]{:S(2)}) copy-start(bf16[1,12,1,1024]{3,2,1,0:T(2,128)(2,1)} %get-tuple-element.64) | copy-start | bytes 73732
  62.2 8.7 %copy-start.81 = (bf16[1,12,1,1024]{3,2,1,0:T(2,128)(2,1)S(1)}, bf16[1,12,1,1024]{3,2,1,0:T(2,128)(2,1)}, u32[]{:S(2)}) copy-start(bf16[1,12,1,1024]{3,2,1,0:T(2,128)(2,1)} %get-tuple-element.65) | copy-start | bytes 73732
  65.6 5.4 %copy-start.64 = (bf16[1,12,1,1024]{3,2,1,0:T(2,128)(2,1)S(1)}, bf16[1,12,1,1024]{3,2,1,0:T(2,128)(2,1)}, u32[]{:S(2)}) copy-start(bf16[1,12,1,1024]{3,2,1,0:T(2,128)(2,1)} %get-tuple-element.57) | copy-start | bytes 73732
  65.6 5.4 %copy-start.68 = (bf16[1,12,1,1024]{3,2,1,0:T(2,128)(2,1)S(1)}, bf16[1,12,1,1024]{3,2,1,0:T(2,128)(2,1)}, u32[]{:S(2)}) copy-start(bf16[1,12,1,1024]{3,2,1,0:T(2,128)(2,1)} %get-tuple-element.58) | copy-start | bytes 73732
  65.6 5.4 %copy-start.75 = (bf16[1,12,1,1024]{3,2,1,0:T(2,128)(2,1)S(1)}, bf16[1,12,1,1024]{3,2,1,0:T(2,128)(2,1)}, u32[]{:S(2)}) copy-start(bf16[1,12,1,1024]{3,2,1,0:T(2,128)(2,1)} %get-tuple-element.59) | copy-start | bytes 73732
  65.6 5.4 %copy-start.80 = (bf16[1,12,1,1024]{3,2,1,0:T(2,128)(2,1)S(1)}, bf16[1,12,1,1024]{3,2,1,0:T(2,128)(2,1)}, u32[]{:S(2)}) copy-start(bf16[1,12,1,1024]{3,2,1,0:T(2,128)(2,1)} %get-tuple-element.60) | copy-start | bytes 73732
  65.6 5.4 %copy-start.83 = (bf16[1,12,1,1024]{3,2,1,0:T(2,128)(2,1)S(1)}, bf16[1,12,1,1024]{3,2,1,0:T(2,128)(2,1)}, u32[]{:S(2)}) copy-start(bf16[1,12,1,1024]{3,2,1,0:T(2,128)(2,1)} %copy-done.82) | copy-start | bytes 73732
  65.6 29.9 %collective-permute-start.2 = (f32[1,5,12,256]{3,2,1,0:T(8,128)}, f32[1,5,12,256]{3,2,1,0:T(8,128)}, u32[]{:S(2)}, u32[]{:S(2)}) collective-permute-start(f32[1,5,12,256]{3,2,1,0:T(8,128)} %fusion.9), channel_id=1, source_target_pairs={{510,0},{0,2},{2,4},{4,6},{6,8},{8,10},{10,12},{12,14},{14,16},{16... | collective-permute-start | bytes 184328 | tf_op jit(solution)/shard_map/ppermute | solution.py:14
  67.7 3.4 %copy-start.5 = (f32[1,5,12,1024]{3,2,1,0:T(8,128)S(1)}, f32[1,5,12,1024]{3,2,1,0:T(8,128)}, u32[]{:S(2)}) copy-start(f32[1,5,12,1024]{3,2,1,0:T(8,128)} %get-tuple-element.16) | copy-start | bytes 737284
  67.7 3.4 %copy-start.71 = (bf16[1,12,1,1024]{3,2,1,0:T(2,128)(2,1)S(1)}, bf16[1,12,1,1024]{3,2,1,0:T(2,128)(2,1)}, u32[]{:S(2)}) copy-start(bf16[1,12,1,1024]{3,2,1,0:T(2,128)(2,1)} %get-tuple-element.50) | copy-start | bytes 73732
  67.7 3.4 %copy-start.77 = (bf16[1,12,1,1024]{3,2,1,0:T(2,128)(2,1)S(1)}, bf16[1,12,1,1024]{3,2,1,0:T(2,128)(2,1)}, u32[]{:S(2)}) copy-start(bf16[1,12,1,1024]{3,2,1,0:T(2,128)(2,1)} %get-tuple-element.55) | copy-start | bytes 73732
  72.0 3.1 %copy-start.87 = (f32[1,1024]{1,0:T(1,128)S(1)}, f32[1,1024]{1,0:T(1,128)}, u32[]{:S(2)}) copy-start(f32[1,1024]{1,0:T(1,128)} %param.14) | copy-start | bytes 12292
  72.1 4.0 %copy-start.6 = (f32[1,5,12,1024]{3,2,1,0:T(8,128)}, f32[1,5,12,1024]{3,2,1,0:T(8,128)S(1)}, u32[]{:S(2)}) copy-start(f32[1,5,12,1024]{3,2,1,0:T(8,128)S(1)} %get-tuple-element.80) | copy-start | bytes 737284
  72.1 4.2 %copy-start.89 = (f32[1,256]{1,0:T(1,128)S(1)}, f32[1,256]{1,0:T(1,128)}, u32[]{:S(2)}) copy-start(f32[1,256]{1,0:T(1,128)} %param.16) | copy-start | bytes 3076
  86.4 2.1 %copy-start.15 = (bf16[1,12,1,1024]{3,2,1,0:T(2,128)(2,1)S(1)}, bf16[1,12,1,1024]{3,2,1,0:T(2,128)(2,1)}, u32[]{:S(2)}) copy-start(bf16[1,12,1,1024]{3,2,1,0:T(2,128)(2,1)} %copy-done.14) | copy-start | bytes 73732
  86.4 2.1 %copy-start.57 = (bf16[1,12,1,1024]{3,2,1,0:T(2,128)(2,1)S(1)}, bf16[1,12,1,1024]{3,2,1,0:T(2,128)(2,1)}, u32[]{:S(2)}) copy-start(bf16[1,12,1,1024]{3,2,1,0:T(2,128)(2,1)} %copy-done.56) | copy-start | bytes 73732
  86.4 2.1 %copy-start.59 = (bf16[1,12,1,1024]{3,2,1,0:T(2,128)(2,1)S(1)}, bf16[1,12,1,1024]{3,2,1,0:T(2,128)(2,1)}, u32[]{:S(2)}) copy-start(bf16[1,12,1,1024]{3,2,1,0:T(2,128)(2,1)} %copy-done.58) | copy-start | bytes 73732
  86.4 2.1 %copy-start.61 = (bf16[1,12,1,1024]{3,2,1,0:T(2,128)(2,1)S(1)}, bf16[1,12,1,1024]{3,2,1,0:T(2,128)(2,1)}, u32[]{:S(2)}) copy-start(bf16[1,12,1,1024]{3,2,1,0:T(2,128)(2,1)} %copy-done.60) | copy-start | bytes 73732
  86.4 2.2 %copy-start.11 = (bf16[1,12,1,1024]{3,2,1,0:T(2,128)(2,1)S(1)}, bf16[1,12,1,1024]{3,2,1,0:T(2,128)(2,1)}, u32[]{:S(2)}) copy-start(bf16[1,12,1,1024]{3,2,1,0:T(2,128)(2,1)} %copy-done.10) | copy-start | bytes 73732
  86.4 2.2 %copy-start.49 = (bf16[1,12,1,1024]{3,2,1,0:T(2,128)(2,1)S(1)}, bf16[1,12,1,1024]{3,2,1,0:T(2,128)(2,1)}, u32[]{:S(2)}) copy-start(bf16[1,12,1,1024]{3,2,1,0:T(2,128)(2,1)} %copy-done.48) | copy-start | bytes 73732
  86.4 2.2 %copy-start.51 = (bf16[1,12,1,1024]{3,2,1,0:T(2,128)(2,1)S(1)}, bf16[1,12,1,1024]{3,2,1,0:T(2,128)(2,1)}, u32[]{:S(2)}) copy-start(bf16[1,12,1,1024]{3,2,1,0:T(2,128)(2,1)} %copy-done.50) | copy-start | bytes 73732
  86.5 2.2 %copy-start.53 = (bf16[1,12,1,1024]{3,2,1,0:T(2,128)(2,1)S(1)}, bf16[1,12,1,1024]{3,2,1,0:T(2,128)(2,1)}, u32[]{:S(2)}) copy-start(bf16[1,12,1,1024]{3,2,1,0:T(2,128)(2,1)} %copy-done.52) | copy-start | bytes 73732
  86.5 2.2 %copy-start.55 = (bf16[1,12,1,1024]{3,2,1,0:T(2,128)(2,1)S(1)}, bf16[1,12,1,1024]{3,2,1,0:T(2,128)(2,1)}, u32[]{:S(2)}) copy-start(bf16[1,12,1,1024]{3,2,1,0:T(2,128)(2,1)} %copy-done.54) | copy-start | bytes 73732
  86.5 2.3 %copy-start.9 = (bf16[1,12,1,1024]{3,2,1,0:T(2,128)(2,1)S(1)}, bf16[1,12,1,1024]{3,2,1,0:T(2,128)(2,1)}, u32[]{:S(2)}) copy-start(bf16[1,12,1,1024]{3,2,1,0:T(2,128)(2,1)} %copy-done.8) | copy-start | bytes 73732
  86.5 2.3 %copy-start.41 = (bf16[1,12,1,1024]{3,2,1,0:T(2,128)(2,1)S(1)}, bf16[1,12,1,1024]{3,2,1,0:T(2,128)(2,1)}, u32[]{:S(2)}) copy-start(bf16[1,12,1,1024]{3,2,1,0:T(2,128)(2,1)} %copy-done.40) | copy-start | bytes 73732
  86.5 2.3 %copy-start.43 = (bf16[1,12,1,1024]{3,2,1,0:T(2,128)(2,1)S(1)}, bf16[1,12,1,1024]{3,2,1,0:T(2,128)(2,1)}, u32[]{:S(2)}) copy-start(bf16[1,12,1,1024]{3,2,1,0:T(2,128)(2,1)} %copy-done.42) | copy-start | bytes 73732
  86.5 2.3 %copy-start.45 = (bf16[1,12,1,1024]{3,2,1,0:T(2,128)(2,1)S(1)}, bf16[1,12,1,1024]{3,2,1,0:T(2,128)(2,1)}, u32[]{:S(2)}) copy-start(bf16[1,12,1,1024]{3,2,1,0:T(2,128)(2,1)} %copy-done.44) | copy-start | bytes 73732
  86.5 2.3 %copy-start.47 = (bf16[1,12,1,1024]{3,2,1,0:T(2,128)(2,1)S(1)}, bf16[1,12,1,1024]{3,2,1,0:T(2,128)(2,1)}, u32[]{:S(2)}) copy-start(bf16[1,12,1,1024]{3,2,1,0:T(2,128)(2,1)} %copy-done.46) | copy-start | bytes 73732
  (48 other events, 64.6 us)
